TPU v7x, 512 devices: a whole 4x4x16 slice. The times are simulated.
512 devices in a mesh: quarter: 4 (over x), row: 8 (over z_lo), col: 16 (over y, z_hi, core).
Axes of the slice: x: 4, y: 4, z: 16 (z_hi: 2, z_lo: 8; z = z_hi * 8 + z_lo), core: 2. Of those that a mesh axis runs over, the one named last changes fastest.
Arguments:
- grad: bfloat16 [4, 4096, 4096], P('quarter', 'row', 'col'), may hold values from -6 to 6
- left_root: bfloat16 [4096, 4096], P('row', 'col'), may hold values from -1 to 3, as said below
- right_root: bfloat16 [4, 4096, 4096], P('quarter', 'row', 'col'), may hold values from -1 to 3, as said below
- momentum: float32 [4, 4096, 4096], P('quarter', 'row', 'col'), may hold values from -6 to 6
- weights: bfloat16 [4, 4096, 4096], P('quarter', 'row', 'col'), may hold values from -6 to 6
Outputs:
- momentum_new: float32 [4, 4096, 4096], P('quarter', 'row', 'col')
- new_weights: bfloat16 [4, 4096, 4096], P(None, ('row', 'quarter'), 'col')
Inputs may be any that keep to these rules, and one draw needn't show every extreme that they name: `left_root`: symmetric. `right_root`: each block symmetric.
All inputs are finite; a program needn't handle non-finite values.
Results may differ from a plain program's by a relative error of at most 0.001.
Values may be sent and summed in bfloat16 or wider, within the bound.
No kernel may reach another device: no remote copies, remote signals or barrier semaphores. Data moves between devices by JAX's collectives and lax.ppermute only.
A program may use at most 64 MiB of HBM per device.

v0:
```python
import jax
import jax.numpy as jnp
from jax import lax
from jax.sharding import PartitionSpec as P

decay_rate = 0.9
step_rate = 0.1


def per_device(grad, left_root, right_root, momentum, weights):
    right_panel = lax.all_gather(right_root, "row", axis=1, tiled=True)[0]
    mixed = jnp.dot(
        lax.all_gather(grad, "col", axis=2, tiled=True)[0],
        right_panel,
        preferred_element_type=jnp.float32,
    ).astype(jnp.bfloat16)
    left_panel = lax.all_gather(left_root, "col", axis=1, tiled=True)
    product = jnp.dot(
        left_panel,
        lax.all_gather(mixed, "row", axis=0, tiled=True),
        preferred_element_type=jnp.float32,
    )
    renewed = decay_rate * momentum[0] + (1.0 - decay_rate) * product
    updated = (weights[0].astype(jnp.float32) - step_rate * renewed).astype(jnp.bfloat16)
    spread = lax.all_to_all(updated[None], "quarter", split_axis=1, concat_axis=0, tiled=True)
    return (renewed[None], spread)


def solution(mesh):
    placed = (
        P("quarter", "row", "col"),
        P("row", "col"),
        P("quarter", "row", "col"),
        P("quarter", "row", "col"),
        P("quarter", "row", "col"),
    )
    return jax.shard_map(
        per_device,
        mesh=mesh,
        in_specs=placed,
        out_specs=(P("quarter", "row", "col"), P(None, ("row", "quarter"), "col")),
        check_vma=False,
    )
```

profile of v0, /device:TPU:8, one launch (start us, length us, event | category | flops | bytes accessed | tf_op | source)
XLA Modules:
  0.0 411.7 jit_solution(7492663751729316780)
XLA Ops:
  7.2 0.0 all-gather.7.cloned.1.call-start
  7.2 0.7 all-gather.7.cloned.1.call-update
  7.9 0.0 all-gather.5.cloned.1.call-start
  7.9 0.7 all-gather.5.cloned.1.call-update
  8.6 0.0 copy-start
  8.7 0.0 all-gather.11.cloned.1.call-start
  8.7 0.7 all-gather.11.cloned.1.call-update
  9.4 0.0 copy-start.1
  9.4 0.0 all-gather.9.cloned.1.call-start
  9.4 75.3 %all-gather.7.cloned.1.call-done = bf16[1,4096,256]{2,1,0:T(8,128)(2,1)} async-done(((bf16[1,512,256]{2,1,0:T(8,128)(2,1)}), bf16[1,4096,256]{2,1,0:T(8,128)(2,1)}) %all-gather.7.cloned.1.call-update) | async-done | bytes 2097168 | tf_op jit(solution)/shard_map/all_gather | solution.py:11
  84.7 116.1 %all-gather.5.cloned.1.call-done = bf16[1,512,4096]{2,1,0:T(8,128)(2,1)} async-done(((bf16[1,512,256]{2,1,0:T(8,128)(2,1)}), bf16[1,512,4096]{2,1,0:T(8,128)(2,1)}) %all-gather.5.cloned.1.call-update) | async-done | bytes 4194320 | tf_op jit(solution)/shard_map/all_gather | solution.py:13
  200.9 4.8 %fusion.5 = bf16[512,256]{1,0:T(8,128)(2,1)} fusion(bf16[1,4096,256]{2,1,0:T(8,128)(2,1)} %all-gather.7.cloned.1.call-done, bf16[1,512,4096]{2,1,0:T(8,128)(2,1)} %all-gather.5.cloned.1.call-done), kind=kOutput, calls=%fused_computation.6 | convolution fusion | flops 1073872896 | bytes 6553600 | tf_op jit(solution)/shard_map/dot_general | solution.py:12
  205.7 0.0 all-gather.9.cloned.1.call-update
  205.7 0.0 copy-done
  205.7 0.2 copy.15
  205.9 0.0 copy-done.1
  205.9 0.1 copy.16
  206.1 110.5 %all-gather.11.cloned.1.call-done = bf16[512,4096]{1,0:T(8,128)(2,1)} async-done(((bf16[512,256]{1,0:T(8,128)(2,1)}), bf16[512,4096]{1,0:T(8,128)(2,1)}) %all-gather.11.cloned.1.call-update) | async-done | bytes 4194320 | tf_op jit(solution)/shard_map/all_gather | solution.py:17
  316.6 68.4 %all-gather.9.cloned.1.call-done = bf16[4096,256]{1,0:T(8,128)(2,1)} async-done(((bf16[512,256]{1,0:T(8,128)(2,1)}), bf16[4096,256]{1,0:T(8,128)(2,1)}) %all-gather.9.cloned.1.call-update) | async-done | bytes 2097168 | tf_op jit(solution)/shard_map/all_gather | solution.py:20
  385.1 4.1 %fusion.4 = f32[512,256]{0,1:T(8,128)S(1)} fusion(bf16[4096,256]{1,0:T(8,128)(2,1)} %all-gather.9.cloned.1.call-done, bf16[512,4096]{1,0:T(8,128)(2,1)} %all-gather.11.cloned.1.call-done, f32[1,512,256]{1,2,0:T(8,128)S(1)} %copy.15), kind=kOutput, calls=%fused_computation.5 | convolution fusion | flops 1074135040 | bytes 7340032 | tf_op jit(solution)/shard_map/dot_general | solution.py:18
  389.2 0.1 fusion.11
  389.3 0.4 copy.17
  389.7 0.5 broadcast.13
  390.2 2.2 reduce
  392.4 0.8 reshape.12
  393.2 4.2 %all-to-all-start = ((bf16[4,2,16384]{2,1,0:T(2,128)(2,1)}), bf16[4,2,16384]{2,1,0:T(2,128)(2,1)S(1)}, u32[]{:S(2)}, u32[]{:S(2)}) async-start(bf16[4,2,16384]{2,1,0:T(2,128)(2,1)} %reshape.12), calls=%async_computation | async-start | bytes 524288 | tf_op jit(solution)/shard_map/all_to_all | solution.py:25
  397.4 1.0 copy.18
  398.4 5.7 %all-to-all-done = bf16[4,2,16384]{2,1,0:T(2,128)(2,1)S(1)} async-done(((bf16[4,2,16384]{2,1,0:T(2,128)(2,1)}), bf16[4,2,16384]{2,1,0:T(2,128)(2,1)S(1)}, u32[]{:S(2)}, u32[]{:S(2)}) %all-to-all-start) | async-done | bytes 262176 | tf_op jit(solution)/shard_map/all_to_all | solution.py:25
  404.1 0.3 reshape.13
  404.4 0.7 copy.19
Async XLA Ops:
  7.2 77.6 %all-gather.7.cloned.1.call-start = ((), (), s32[]{:S(2)}) async-start(), calls=%async_computation.2 | async-start | bytes 2359296 | tf_op jit(solution)/shard_map/all_gather | solution.py:11
  7.9 193.0 %all-gather.5.cloned.1.call-start = ((), (), s32[]{:S(2)}) async-start(), calls=%async_computation.1 | async-start | bytes 4456448 | tf_op jit(solution)/shard_map/all_gather | solution.py:13
  8.6 197.1 %copy-start = (f32[1,512,256]{2,1,0:T(8,128)S(1)}, f32[1,512,256]{2,1,0:T(8,128)}, u32[]{:S(2)}) copy-start(f32[1,512,256]{2,1,0:T(8,128)} %param.8) | copy-start | bytes 1572868
  8.7 307.9 %all-gather.11.cloned.1.call-start = ((), (), s32[]{:S(2)}) async-start(), calls=%async_computation.4 | async-start | bytes 4456448 | tf_op jit(solution)/shard_map/all_gather | solution.py:17
  9.4 196.5 %copy-start.1 = (bf16[1,512,256]{2,1,0:T(8,128)(2,1)S(1)}, bf16[1,512,256]{2,1,0:T(8,128)(2,1)}, u32[]{:S(2)}) copy-start(bf16[1,512,256]{2,1,0:T(8,128)(2,1)} %param.9) | copy-start | bytes 786436
  9.4 375.6 %all-gather.9.cloned.1.call-start = ((), (), s32[]{:S(2)}) async-start(), calls=%async_computation.3 | async-start | bytes 2359296 | tf_op jit(solution)/shard_map/all_gather | solution.py:20
  393.2 10.9 %all-to-all-start = ((bf16[4,2,16384]{2,1,0:T(2,128)(2,1)}), bf16[4,2,16384]{2,1,0:T(2,128)(2,1)S(1)}, u32[]{:S(2)}, u32[]{:S(2)}) async-start(bf16[4,2,16384]{2,1,0:T(2,128)(2,1)} %reshape.12), calls=%async_computation | async-start | bytes 524288 | tf_op jit(solution)/shard_map/all_to_all | solution.py:25
Sparse Core Ops, SparseCore 0:
  10.1 74.6 all-gather.6
  87.8 112.9 all-gather.4
  204.0 112.5 all-gather.10
  319.1 65.8 all-gather.8
where the time goes:
time: 412 us
  waiting for transfers between devices  378 us (92%)
  between operations  13.9 us (3%)
  matrix products  8.94 us (2%)
  starting transfers between devices  4.4 us (1%)
    all_gather x1, waiting for transfers between devices, per_device(): lax.all_gather(grad, 'col', axis=2, tiled=True)[0]  116 us
    all_gather x1, waiting for transfers between devices, per_device(): left_panel = lax.all_gather(left_root, 'col', axis=1, tiled=True)  111 us
    all_gather x1, waiting for transfers between devices, per_device(): right_panel = lax.all_gather(right_root, 'row', axis=1, tiled=True)[0]  75.3 us
    all_gather x1, waiting for transfers between devices, per_device(): lax.all_gather(mixed, 'row', axis=0, tiled=True)  68.4 us
  transfers between devices with their start and end apart: 5, of which 5 were waited for; matrix products, arithmetic and copies ran while one was open for 1% of the time, Pallas kernels for 0%

commit v1 on v0

--- a/solution.py
+++ b/solution.py
@@ -8,7 +8,9 @@
 
 
 def per_device(grad, left_root, right_root, momentum, weights):
-    right_panel = lax.all_gather(right_root, "row", axis=1, tiled=True)[0]
+    right_panel = jnp.concatenate(
+        lax.all_to_all(jnp.stack([right_root] * lax.axis_size("row")), "row", 0, 0), axis=1
+    )[0]
     mixed = jnp.dot(
         lax.all_gather(grad, "col", axis=2, tiled=True)[0],
         right_panel,

time: 412 us -> 388 us (0.942)
  waiting for transfers between devices: 378 us -> 189 us
  blocking collectives: 0 us -> 165 us
    all_to_all x0 -> x1, blocking collectives: none -> 165 us  [per_device(): lax.all_to_all(jnp.stack([right_root] * lax.axis_size('row')), 'row', 0, 0)]
    all_gather x1, waiting for transfers between devices: 116 us -> 0.01 us  [per_device(): lax.all_gather(grad, 'col', axis=2, tiled=True)[0]]
    all_gather x1 -> x0, waiting for transfers between devices: 75.3 us -> none  [per_device(): right_panel = lax.all_gather(right_root, 'row', axis=1, tiled=True)[0]]
  transfers between devices with their start and end apart: 5 -> 4, of which waited for: 5 -> 3; matrix products, arithmetic and copies ran while one was open for 1% -> 2% of each run, Pallas kernels for 0% -> 0%
where the time goes in v1:
time: 388 us
  waiting for transfers between devices  189 us (49%)
  blocking collectives  165 us (43%)
  between operations  13.8 us (4%)
  matrix products  8.34 us (2%)
  local copies, waits for them, and re-layouts  5.14 us (1%)
  starting transfers between devices  4.36 us (1%)
    all_to_all x1, blocking collectives, per_device(): lax.all_to_all(jnp.stack([right_root] * lax.axis_size('row')), 'row', 0, 0)  165 us
    all_gather x1, waiting for transfers between devices, per_device(): left_panel = lax.all_gather(left_root, 'col', axis=1, tiled=True)  113 us
    all_gather x1, waiting for transfers between devices, per_device(): lax.all_gather(mixed, 'row', axis=0, tiled=True)  68.6 us
  transfers between devices with their start and end apart: 4, of which 3 were waited for; matrix products, arithmetic and copies ran while one was open for 2% of the time, Pallas kernels for 0%

profile of v1, /device:TPU:8, one launch (start us, length us, event | category | flops | bytes accessed | tf_op | source)
XLA Modules:
  0.0 387.5 jit_solution(6214542115759843097)
XLA Ops:
  7.2 0.0 all-gather.4.cloned.1.call-start
  7.2 0.7 all-gather.4.cloned.1.call-update
  7.9 0.0 all-gather.8.cloned.1.call-start
  7.9 0.7 all-gather.8.cloned.1.call-update
  8.6 0.0 all-gather.6.cloned.1.call-start
  8.7 1.1 stack.2
  9.8 164.6 %all_to_all.17 = bf16[8,1,512,256]{3,2,1,0:T(8,128)(2,1)S(1)} all-to-all(bf16[8,1,512,256]{3,2,1,0:T(8,128)(2,1)S(1)} %stack.2), channel_id=1, replica_groups=mesh['quarter'=4,'row'=8,'col'=16] {'row'}, dimensions={0} | all-to-all | bytes 4194304 | tf_op jit(solution)/shard_map/all_to_all | solution.py:12
  174.4 0.0 all-gather.4.cloned.1.call-done
  174.4 0.0 copy-start
  174.4 0.0 copy-start.1
  174.4 4.2 %fusion.4 = bf16[512,256]{1,0:T(8,128)(2,1)} fusion(bf16[4096,256]{1,0:T(8,128)(2,1)S(1)} %bitcast.26, bf16[1,512,4096]{2,1,0:T(8,128)(2,1)} %all-gather.4.cloned.1.call-done), kind=kOutput, calls=%fused_computation.5 | convolution fusion | flops 1073872896 | bytes 6553600 | tf_op jit(solution)/shard_map/dot_general | solution.py:14
  178.6 0.0 all-gather.6.cloned.1.call-update
  178.7 0.0 copy-done
  178.7 0.2 copy.15
  178.9 0.0 copy-done.1
  178.9 0.1 copy.16
  179.0 113.2 %all-gather.8.cloned.1.call-done = bf16[512,4096]{1,0:T(8,128)(2,1)} async-done(((bf16[512,256]{1,0:T(8,128)(2,1)}), bf16[512,4096]{1,0:T(8,128)(2,1)}) %all-gather.8.cloned.1.call-update) | async-done | bytes 4194320 | tf_op jit(solution)/shard_map/all_gather | solution.py:19
  292.3 68.6 %all-gather.6.cloned.1.call-done = bf16[4096,256]{1,0:T(8,128)(2,1)} async-done(((bf16[512,256]{1,0:T(8,128)(2,1)}), bf16[4096,256]{1,0:T(8,128)(2,1)}) %all-gather.6.cloned.1.call-update) | async-done | bytes 2097168 | tf_op jit(solution)/shard_map/all_gather | solution.py:22
  360.9 4.1 %fusion.3 = f32[512,256]{0,1:T(8,128)S(1)} fusion(bf16[4096,256]{1,0:T(8,128)(2,1)} %all-gather.6.cloned.1.call-done, bf16[512,4096]{1,0:T(8,128)(2,1)} %all-gather.8.cloned.1.call-done, f32[1,512,256]{1,2,0:T(8,128)S(1)} %copy.15), kind=kOutput, calls=%fused_computation.4 | convolution fusion | flops 1074135040 | bytes 7340032 | tf_op jit(solution)/shard_map/dot_general | solution.py:20
  365.0 0.1 fusion.8
  365.1 0.4 copy.17
  365.5 0.5 broadcast.16
  366.1 2.2 reduce
  368.3 0.8 reshape.15
  369.0 4.2 %all-to-all-start.1 = ((bf16[4,2,16384]{2,1,0:T(2,128)(2,1)}), bf16[4,2,16384]{2,1,0:T(2,128)(2,1)S(1)}, u32[]{:S(2)}, u32[]{:S(2)}) async-start(bf16[4,2,16384]{2,1,0:T(2,128)(2,1)} %reshape.15), calls=%async_computation.1 | async-start | bytes 524288 | tf_op jit(solution)/shard_map/all_to_all | solution.py:27
  373.3 1.0 copy.18
  374.3 5.7 %all-to-all-done.1 = bf16[4,2,16384]{2,1,0:T(2,128)(2,1)S(1)} async-done(((bf16[4,2,16384]{2,1,0:T(2,128)(2,1)}), bf16[4,2,16384]{2,1,0:T(2,128)(2,1)S(1)}, u32[]{:S(2)}, u32[]{:S(2)}) %all-to-all-start.1) | async-done | bytes 262176 | tf_op jit(solution)/shard_map/all_to_all | solution.py:27
  380.0 0.3 reshape.16
  380.2 0.7 copy.19
Async XLA Ops:
  7.2 167.3 %all-gather.4.cloned.1.call-start = ((), (), s32[]{:S(2)}) async-start(), calls=%async_computation.2 | async-start | bytes 4456448 | tf_op jit(solution)/shard_map/all_gather | solution.py:15
  7.9 284.4 %all-gather.8.cloned.1.call-start = ((), (), s32[]{:S(2)}) async-start(), calls=%async_computation.4 | async-start | bytes 4456448 | tf_op jit(solution)/shard_map/all_gather | solution.py:19
  8.6 352.2 %all-gather.6.cloned.1.call-start = ((), (), s32[]{:S(2)}) async-start(), calls=%async_computation.3 | async-start | bytes 2359296 | tf_op jit(solution)/shard_map/all_gather | solution.py:22
  174.4 4.2 %copy-start = (f32[1,512,256]{2,1,0:T(8,128)S(1)}, f32[1,512,256]{2,1,0:T(8,128)}, u32[]{:S(2)}) copy-start(f32[1,512,256]{2,1,0:T(8,128)} %param.8) | copy-start | bytes 1572868
  174.4 4.5 %copy-start.1 = (bf16[1,512,256]{2,1,0:T(8,128)(2,1)S(1)}, bf16[1,512,256]{2,1,0:T(8,128)(2,1)}, u32[]{:S(2)}) copy-start(bf16[1,512,256]{2,1,0:T(8,128)(2,1)} %param.9) | copy-start | bytes 786436
  369.0 10.9 %all-to-all-start.1 = ((bf16[4,2,16384]{2,1,0:T(2,128)(2,1)}), bf16[4,2,16384]{2,1,0:T(2,128)(2,1)S(1)}, u32[]{:S(2)}, u32[]{:S(2)}) async-start(bf16[4,2,16384]{2,1,0:T(2,128)(2,1)} %reshape.15), calls=%async_computation.1 | async-start | bytes 524288 | tf_op jit(solution)/shard_map/all_to_all | solution.py:27
Sparse Core Ops, SparseCore 0:
  11.1 121.5 all-gather.3
  135.8 156.3 all-gather.7
  294.9 65.8 all-gather.5
